TPU v7x, 32 devices: a whole 2x2x4 slice. The times are simulated.
32 devices in a mesh: grp: 2 (over x), gx: 16 (over z, y, core).
Axes of the slice: x: 2, y: 2, z: 4, core: 2. Of those that a mesh axis runs over, the one named last changes fastest.
Arguments:
- prompt_rows: bfloat16 [4096, 16384], P(('grp', 'gx')), parts along dimension 0, may hold values from -6 to 6
- decode_rows: bfloat16 [64, 16384], P(('grp', 'gx')), parts along dimension 0, may hold values from -6 to 6
- norm_gain: bfloat16 [16384], replicated, may hold values from 0.25 to 1.75
- w_query: bfloat16 [16384, 8192], P(None, 'gx'), may hold values from -0.046875 to 0.046875
- w_key: bfloat16 [16384, 512], P('gx'), may hold values from -0.046875 to 0.046875
- w_value: bfloat16 [16384, 512], P('gx'), may hold values from -0.046875 to 0.046875
- key_cache: bfloat16 [64, 4, 256, 128], P(('grp', 'gx')), parts along dimension 0, may hold values from -6 to 6
- value_cache: bfloat16 [64, 4, 256, 128], P(('grp', 'gx')), parts along dimension 0, may hold values from -6 to 6
- positions: int32 [4096], P(('grp', 'gx')), parts along dimension 0, may hold values from 0 to 8191, as said below
- lengths: int32 [64], P('grp'), parts along dimension 0, may hold values from 1 to 256, 3276 in all
- slots: int32 [32], P('grp'), parts along dimension 0, may hold values from 0 to 31, as said below
Outputs:
- prompt_keys: bfloat16 [4096, 512], P(('grp', 'gx')), parts along dimension 0
- attended: bfloat16 [64, 8192], P(('grp', 'gx')), parts along dimension 0
There are 2 independent parts, one for each index of `grp`. A program takes and returns all parts, laid end to end along the dimension named above; an argument that names none is the same for every part. Nothing has to cross between parts.
Inputs may be any that keep to these rules, and one draw needn't show every extreme that they name: The positions of each span are consecutive. The slots are distinct.
All inputs are finite; a program needn't handle non-finite values.
Results may differ from a plain program's by a relative error of at most 0.007.
Values may be sent and summed in bfloat16 or wider, within the bound.
No kernel may reach another device: no remote copies, remote signals or barrier semaphores. Data moves between devices by JAX's collectives and lax.ppermute only.
A program may use at most 128 MiB of HBM per device.

v0:
```python
import math

import jax
import jax.numpy as jnp
from jax import lax
from jax.sharding import PartitionSpec as P

THETA = 500000.0
EPSILON = 1e-05


def normalize(values, gain):
    wide = values.astype(jnp.float32)
    square_mean = jnp.mean(wide * wide, axis=-1, keepdims=True)
    return (wide * lax.rsqrt(square_mean + EPSILON) * gain.astype(jnp.float32)).astype(jnp.bfloat16)


def rotate(vectors, places):
    head_size = vectors.shape[-1]
    half_size = head_size // 2
    exponent = jnp.arange(half_size).astype(jnp.float32) * (2.0 / head_size)
    inverse = jnp.power(jnp.float32(THETA), -exponent)
    angles = places.astype(jnp.float32)[:, None] * inverse[None, :]
    cosine = jnp.cos(angles)[:, None, :]
    sine = jnp.sin(angles)[:, None, :]
    first = vectors[..., :half_size]
    second = vectors[..., half_size:]
    return jnp.concatenate(
        [first * cosine - second * sine, second * cosine + first * sine], axis=-1
    )


def attend(grouped, key_block, value_block, fresh_keys, fresh_values, live_lengths):
    scale_factor = 1.0 / math.sqrt(grouped.shape[-1])
    scores = (
        jnp.einsum("bgqd,bgtd->bgqt", grouped, key_block, preferred_element_type=jnp.float32)
        * scale_factor
    )
    own_scores = (
        jnp.einsum("bgqd,bgd->bgq", grouped, fresh_keys, preferred_element_type=jnp.float32)
        * scale_factor
    )
    live = jnp.arange(key_block.shape[2])[None, :] < live_lengths[:, None]
    weights = jnp.where(live[:, None, None, :], jnp.exp(scores), jnp.float32(0.0))
    own_weight = jnp.exp(own_scores)
    total = jnp.sum(weights, axis=-1) + own_weight
    shares = (weights / total[..., None]).astype(jnp.bfloat16)
    own_share = (own_weight / total).astype(jnp.bfloat16)
    mixed = jnp.einsum("bgqt,bgtd->bgqd", shares, value_block, preferred_element_type=jnp.float32)
    mixed = (
        mixed
        + own_share.astype(jnp.float32)[..., None] * fresh_values.astype(jnp.float32)[:, :, None, :]
    )
    return mixed


def per_device(
    prompt_rows,
    decode_rows,
    norm_gain,
    w_query,
    w_key,
    w_value,
    key_cache,
    value_cache,
    positions,
    lengths,
    slots,
):
    span_rows = prompt_rows.shape[0]
    shard_rows = w_key.shape[0]
    key_columns = w_key.shape[1]
    kv_heads = key_cache.shape[1]
    head_size = key_cache.shape[3]
    own_rows = decode_rows.shape[0]
    prompt_normed = normalize(prompt_rows, norm_gain)
    features = prompt_normed
    key_sums = jnp.dot(
        features,
        lax.all_gather(w_key, "gx", axis=0, tiled=True),
        preferred_element_type=jnp.float32,
    )
    prompt_keys = rotate(key_sums.reshape(span_rows, kv_heads, head_size), positions)
    prompt_keys = prompt_keys.reshape(span_rows, key_columns).astype(jnp.bfloat16)
    decode_normed = normalize(decode_rows, norm_gain)
    final_row = prompt_normed[span_rows - 1 :]
    every_row = lax.all_gather(decode_normed, "gx", axis=0, tiled=True)
    finals = lax.all_gather(final_row, "gx", axis=0, tiled=True)
    every_row = every_row.at[slots].set(finals)
    total_rows = every_row.shape[0]
    heads_here = w_query.shape[1] // head_size
    query_sums = jnp.dot(every_row, w_query, preferred_element_type=jnp.float32).reshape(
        total_rows, heads_here, head_size
    )
    queries = (
        rotate(query_sums, lengths).reshape(total_rows, heads_here * head_size).astype(jnp.bfloat16)
    )
    own_queries = lax.all_to_all(queries, "gx", split_axis=0, concat_axis=1, tiled=True)
    feature_start = lax.axis_index("gx") * shard_rows
    features = lax.dynamic_slice_in_dim(every_row, feature_start, shard_rows, 1)
    key_part = jnp.dot(features, w_key, preferred_element_type=jnp.float32)
    value_part = jnp.dot(features, w_value, preferred_element_type=jnp.float32)
    fresh = lax.psum_scatter(
        jnp.concatenate([key_part, value_part], axis=1), "gx", scatter_dimension=0, tiled=True
    )
    own_lengths = lax.dynamic_slice_in_dim(lengths, lax.axis_index("gx") * own_rows, own_rows, 0)
    new_keys = rotate(
        fresh[:, :key_columns].reshape(own_rows, kv_heads, head_size), own_lengths
    ).astype(jnp.bfloat16)
    new_values = fresh[:, key_columns:].reshape(own_rows, kv_heads, head_size).astype(jnp.bfloat16)
    all_heads = own_queries.shape[1] // head_size
    grouped = own_queries.reshape(own_rows, kv_heads, all_heads // kv_heads, head_size)
    mixed = attend(grouped, key_cache, value_cache, new_keys, new_values, own_lengths)
    attended = mixed.reshape(own_rows, all_heads * head_size).astype(jnp.bfloat16)
    return (prompt_keys, attended)


def solution(mesh):
    return jax.shard_map(
        per_device,
        mesh=mesh,
        in_specs=(
            P(("grp", "gx"), None),
            P(("grp", "gx"), None),
            P(),
            P(None, "gx"),
            P("gx", None),
            P("gx", None),
            P(("grp", "gx"), None, None, None),
            P(("grp", "gx"), None, None, None),
            P(("grp", "gx")),
            P("grp"),
            P("grp"),
        ),
        out_specs=(P(("grp", "gx"), None), P(("grp", "gx"), None)),
        check_vma=False,
    )
```

profile of v0, /device:TPU:0, one launch (start us, length us, event | category | flops | bytes accessed | tf_op | source)
XLA Modules:
  0.0 293.5 jit_solution(4164179488035033427)
XLA Ops:
  7.2 0.0 copy-start
  7.2 0.0 copy-start.6
  7.2 0.0 all-gather.7.cloned.1.call-start
  7.2 0.8 convert_element_type.80
  8.1 1.1 fusion.9
  9.2 1.6 fusion.13
  10.8 0.0 all-gather.7.cloned.1.call-update
  10.8 0.0 all-reduce.3.cloned.1.call-start
  10.9 3.1 %fusion = f32[128]{0:T(128)S(1)} fusion(bf16[128,16384]{1,0:T(8,128)(2,1)} %param.11), kind=kLoop, calls=%fused_computation.3 | loop fusion | flops 6291328 | bytes 4194816 | tf_op jit(solution)/shard_map/reduce_sum | solution.py:14
  13.9 0.0 copy-start.2
  14.0 0.0 copy-start.7
  14.0 0.0 copy-start.4
  14.0 3.5 %fusion.2 = bf16[128,16384]{1,0:T(8,128)(2,1)S(1)} fusion(bf16[128,16384]{1,0:T(8,128)(2,1)} %param.11, f32[16384]{0:T(1024)S(1)} %convert_element_type.80, f32[128]{0:T(128)S(1)} %add_rsqrt_fusion.1), kind=kLoop, calls=%fused_computation.5 | loop fusion | flops 8388608 | bytes 8454656 | tf_op jit(solution)/shard_map/convert_element_type | solution.py:15
  17.5 0.0 copy-start.1
  17.5 1.9 copy-done.1
  19.4 0.1 slice_bitcast_fusion
  19.5 0.0 copy-done.6
  19.5 27.9 %all-gather.1 = bf16[16,1,16384]{2,1,0:T(2,128)(2,1)} all-gather(bf16[1,1,16384]{2,1,0:T(2,128)(2,1)S(1)} %slice_bitcast_fusion), channel_id=1, replica_groups=mesh['grp'=2,'gx'=16] {'gx'}, dimensions={0}, use_global_device_ids=true | all-gather | bytes 557056 | tf_op jit(solution)/shard_map/all_gather | solution.py:88
  47.4 5.5 %all-gather.7.cloned.1.call-done = bf16[16,2,16384]{2,1,0:T(2,128)(2,1)} async-done(((bf16[1,2,16384]{2,1,0:T(2,128)(2,1)}), bf16[16,2,16384]{2,1,0:T(2,128)(2,1)}) %all-gather.7.cloned.1.call-update) | async-done | bytes 1048592 | tf_op jit(solution)/shard_map/all_gather | solution.py:87
  52.9 1.5 reshape.230
  54.4 3.1 %scatter_custom_fusion = bf16[32,16384]{1,0:T(8,128)(2,1)S(1)} fusion(bf16[32,16384]{1,0:T(8,128)(2,1)S(1)} %reshape.230, s32[16]{0:T(128)S(1)} %compare_select_fusion, bf16[16,1,16384]{2,1,0:T(2,128)(2,1)} %all-gather.1), kind=kCustom, calls=%fused_computation.11 | custom fusion | bytes 1572864 | tf_op jit(solution)/shard_map/scatter | solution.py:89
  57.5 0.0 copy-done
  57.5 0.3 fusion.14
  57.8 0.0 copy-done.2
  57.8 0.3 fusion.16
  58.1 0.7 pad_maximum_fusion.1
  58.8 0.0 all-reduce.3.cloned.1.call-update
  58.8 0.0 all-gather.5.cloned.1.call-start
  58.8 0.7 all-gather.5.cloned.1.call-update
  59.5 0.0 copy-done.7
  59.6 0.0 copy-done.4
  59.6 0.1 fusion.25
  59.7 0.1 multiply_cosine_fusion.2
  59.8 0.1 multiply_cosine_fusion.1
  59.9 0.3 multiply_cosine_fusion
  60.2 0.0 copy-start.8
  60.3 0.0 copy-start.3
  60.3 0.0 copy-start.5
  60.3 8.8 %fusion.28 = f32[32,512]{1,0:T(8,128)S(1)} fusion(bf16[32,16384]{1,0:T(8,128)(2,1)S(1)} %scatter_custom_fusion, bf16[16384,512]{1,0:T(8,128)(2,1)} %param.14), kind=kOutput, calls=%fused_computation.64 | convolution fusion | flops 536870912 | bytes 17891328 | tf_op jit(solution)/shard_map/dot_general | solution.py:92
  69.2 0.1 subtract_convert_fusion.1
  69.3 0.1 pad_maximum_fusion.2
  69.4 0.6 convert_element_type.88
  70.0 3.6 %all-to-all-start = ((bf16[16,2,512]{2,1,0:T(2,128)(2,1)}), bf16[16,2,512]{2,1,0:T(2,128)(2,1)S(1)}, u32[]{:S(2)}, u32[]{:S(2)}) async-start(bf16[16,2,512]{2,1,0:T(2,128)(2,1)} %convert_element_type.88), calls=%async_computation | async-start | bytes 65536 | tf_op jit(solution)/shard_map/all_to_all | solution.py:98
  73.6 0.1 iota_compare_fusion
  73.7 0.0 copy-done.8
  73.7 0.6 dynamic-slice
  75.0 5.3 %all-to-all-done = bf16[16,2,512]{2,1,0:T(2,128)(2,1)S(1)} async-done(((bf16[16,2,512]{2,1,0:T(2,128)(2,1)}), bf16[16,2,512]{2,1,0:T(2,128)(2,1)S(1)}, u32[]{:S(2)}, u32[]{:S(2)}) %all-to-all-start) | async-done | bytes 32800 | tf_op jit(solution)/shard_map/all_to_all | solution.py:98
  80.3 0.0 copy-done.3
  80.4 0.3 fusion.26
  80.7 65.5 %all-reduce.3.cloned.1.call-done = f32[32,1024]{1,0:T(8,128)} async-done(((f32[32,1024]{1,0:T(8,128)}), f32[32,1024]{1,0:T(8,128)}) %all-reduce.3.cloned.1.call-update) | async-done | bytes 131088
  146.2 0.7 constant_dynamic-slice_fusion
  146.9 0.8 fusion.21
  147.7 0.1 subtract_convert_fusion.2
  147.8 0.1 maximum_bitcast_fusion
  147.9 0.1 fusion.18
  148.0 0.0 copy-done.5
  148.0 0.2 fusion.5
  148.3 0.7 copy.30
  148.9 127.4 %all-gather.5.cloned.1.call-done = bf16[16384,512]{1,0:T(8,128)(2,1)} async-done(((bf16[1024,512]{1,0:T(8,128)(2,1)}), bf16[16384,512]{1,0:T(8,128)(2,1)}) %all-gather.5.cloned.1.call-update) | async-done | bytes 16777232 | tf_op jit(solution)/shard_map/all_gather | solution.py:80
  276.3 9.4 %fusion.27 = f32[128,512]{1,0:T(8,128)S(1)} fusion(bf16[128,16384]{1,0:T(8,128)(2,1)} %copy-done.1, bf16[16384,512]{1,0:T(8,128)(2,1)} %all-gather.5.cloned.1.call-done), kind=kOutput, calls=%fused_computation.63 | convolution fusion | flops 2147483648 | bytes 21233664 | tf_op jit(solution)/shard_map/dot_general | solution.py:78
  285.7 0.1 reshape.215
  285.8 0.3 subtract_convert_fusion
  286.1 0.2 pad_maximum_fusion
  286.3 0.7 copy.29
  (12 shorter events, 0.2 us)
Async XLA Ops:
  7.2 50.4 %copy-start = (bf16[1024,512]{1,0:T(8,128)(2,1)S(1)}, bf16[1024,512]{1,0:T(8,128)(2,1)}, u32[]{:S(2)}) copy-start(bf16[1024,512]{1,0:T(8,128)(2,1)} %param.16) | copy-start | bytes 3145732
  7.2 12.3 %copy-start.6 = (s32[16]{0:T(128)S(1)}, s32[16]{0:T(128)}, u32[]{:S(2)}) copy-start(s32[16]{0:T(128)} %param.21) | copy-start | bytes 196
  7.2 45.8 %all-gather.7.cloned.1.call-start = ((), (), s32[]{:S(2)}) async-start(), calls=%async_computation.2 | async-start | bytes 1114112 | tf_op jit(solution)/shard_map/all_gather | solution.py:87
  10.8 135.4 %all-reduce.3.cloned.1.call-start = ((), (), s32[]{:S(2)}) async-start(), calls=%async_computation.3 | async-start | bytes 262144
  13.9 43.9 %copy-start.2 = (bf16[1024,512]{1,0:T(8,128)(2,1)S(1)}, bf16[1024,512]{1,0:T(8,128)(2,1)}, u32[]{:S(2)}) copy-start(bf16[1024,512]{1,0:T(8,128)(2,1)} %param.15) | copy-start | bytes 3145732
  14.0 45.6 %copy-start.7 = (s32[128]{0:T(128)S(1)}, s32[128]{0:T(128)}, u32[]{:S(2)}) copy-start(s32[128]{0:T(128)} %param.19) | copy-start | bytes 1540
  14.0 45.6 %copy-start.4 = (s32[32]{0:T(128)S(1)}, s32[32]{0:T(128)}, u32[]{:S(2)}) copy-start(s32[32]{0:T(128)} %param.20) | copy-start | bytes 388
  17.5 1.9 copy-start.1
  58.8 217.5 %all-gather.5.cloned.1.call-start = ((), (), s32[]{:S(2)}) async-start(), calls=%async_computation.1 | async-start | bytes 17825792 | tf_op jit(solution)/shard_map/all_gather | solution.py:80
  60.2 13.5 %copy-start.8 = (u32[32]{0:T(128)S(1)}, u32[32]{0:T(128)}, u32[]{:S(2)}) copy-start(u32[32]{0:T(128)} %constant.38) | copy-start | bytes 388
  60.3 20.1 %copy-start.3 = (bf16[2,4,256,128]{3,2,1,0:T(8,128)(2,1)S(1)}, bf16[2,4,256,128]{3,2,1,0:T(8,128)(2,1)}, u32[]{:S(2)}) copy-start(bf16[2,4,256,128]{3,2,1,0:T(8,128)(2,1)} %param.17) | copy-start | bytes 1572868
  60.3 87.8 %copy-start.5 = (bf16[2,4,256,128]{3,2,1,0:T(8,128)(2,1)S(1)}, bf16[2,4,256,128]{3,2,1,0:T(8,128)(2,1)}, u32[]{:S(2)}) copy-start(bf16[2,4,256,128]{3,2,1,0:T(8,128)(2,1)} %param.18) | copy-start | bytes 1572868
  70.0 10.3 %all-to-all-start = ((bf16[16,2,512]{2,1,0:T(2,128)(2,1)}), bf16[16,2,512]{2,1,0:T(2,128)(2,1)S(1)}, u32[]{:S(2)}, u32[]{:S(2)}) async-start(bf16[16,2,512]{2,1,0:T(2,128)(2,1)} %convert_element_type.88), calls=%async_computation | async-start | bytes 65536 | tf_op jit(solution)/shard_map/all_to_all | solution.py:98
Sparse Core Ops, SparseCore 0:
  10.9 41.9 all-gather.6
  58.9 87.1 all-reduce.2
  148.3 127.9 all-gather.4
where the time goes:
time: 294 us
  waiting for transfers between devices  204 us (69%)
  blocking collectives  27.9 us (9%)
  matrix products  19.5 us (7%)
  between operations  14.7 us (5%)
  other arithmetic  13.2 us (4%)
  local copies, waits for them, and re-layouts  10.2 us (3%)
  starting transfers between devices  3.76 us (1%)
    all_gather x1, waiting for transfers between devices, per_device(): lax.all_gather(w_key, 'gx', axis=0, tiled=True)  127 us
    unnamed x4, waiting for transfers between devices  66.2 us
    all_gather x1, blocking collectives, per_device(): finals = lax.all_gather(final_row, 'gx', axis=0, tiled=True)  27.9 us
    dot_general x1, matrix products, per_device(): jnp.dot(features, lax.all_gather(w_key, 'gx', axis=0, tiled=True), prefer...  9.38 us
    dot_general x1, matrix products, per_device(): jnp.dot(every_row, w_query, preferred_element_type=jnp.float32)  8.83 us
  transfers between devices with their start and end apart: 4, of which 4 were waited for; matrix products, arithmetic and copies ran while one was open for 7% of the time, Pallas kernels for 0%

commit v1 on v0

v1 whole, which is shorter than its diff:
```python
import functools
import math

import jax
import jax.numpy as jnp
from jax import lax
from jax.experimental import pallas as pl
from jax.experimental.pallas import tpu as pltpu
from jax.sharding import PartitionSpec as P

THETA = 500000.0
EPSILON = 1e-05
LANES = 128
CORES = 2
PLANE = 4
BOTH = ("grp", "gx")


class Grid:
    def __init__(self, mesh, shard_rows):
        self.parts = mesh.shape["grp"]
        self.count = mesh.shape["gx"]
        self.ys = max(1, PLANE // self.parts)
        self.zs = self.count // (self.ys * CORES)
        pair = self.parts % 2 == 0 and shard_rows % (2 * LANES) == 0
        self.pair = 2 if pair else 1
        self.sub = shard_rows // self.pair

    def place(self, g, z, y, c):
        return g * self.count + (z * self.ys + y) * CORES + c

    def perm(self, dg=0, dz=0, dy=0, dc=0):
        moves = []
        for g in range(self.parts):
            low = g % self.pair
            other = g - low + (low + dg) % self.pair
            for z in range(self.zs):
                for y in range(self.ys):
                    for c in range(CORES):
                        there = self.place(
                            other, (z + dz) % self.zs, (y + dy) % self.ys, (c + dc) % CORES
                        )
                        moves.append((self.place(g, z, y, c), there))
        return moves

    def send(self, value, **offsets):
        return lax.ppermute(value, BOTH, self.perm(**offsets))


def normalize(values, gain):
    wide = values.astype(jnp.float32)
    square_mean = jnp.mean(wide * wide, axis=-1, keepdims=True)
    return (wide * lax.rsqrt(square_mean + EPSILON) * gain.astype(jnp.float32)).astype(jnp.bfloat16)


def angles_of(places, head_size):
    half_size = head_size // 2
    exponent = jnp.arange(half_size).astype(jnp.float32) * (2.0 / head_size)
    inverse = jnp.power(jnp.float32(THETA), -exponent)
    angles = places.astype(jnp.float32)[:, None] * inverse[None, :]
    cosine, sine = jnp.cos(angles), jnp.sin(angles)
    return jnp.concatenate([cosine, cosine], -1), jnp.concatenate([-sine, sine], -1)


def rotate(vectors, cosine, sine):
    half_size = vectors.shape[-1] // 2
    swapped = jnp.concatenate([vectors[..., half_size:], vectors[..., :half_size]], axis=-1)
    return vectors * cosine[:, None, :] + swapped * sine[:, None, :]


def attend(grouped, key_block, value_block, fresh_keys, fresh_values, live_lengths):
    scale_factor = 1.0 / math.sqrt(grouped.shape[-1])
    scores = (
        jnp.einsum("bgqd,bgtd->bgqt", grouped, key_block, preferred_element_type=jnp.float32)
        * scale_factor
    )
    own_scores = (
        jnp.einsum("bgqd,bgd->bgq", grouped, fresh_keys, preferred_element_type=jnp.float32)
        * scale_factor
    )
    live = jnp.arange(key_block.shape[2])[None, :] < live_lengths[:, None]
    weights = jnp.where(live[:, None, None, :], jnp.exp(scores), jnp.float32(0.0))
    own_weight = jnp.exp(own_scores)
    total = jnp.sum(weights, axis=-1) + own_weight
    shares = (weights / total[..., None]).astype(jnp.bfloat16)
    own_share = (own_weight / total).astype(jnp.bfloat16)
    mixed = jnp.einsum("bgqt,bgtd->bgqd", shares, value_block, preferred_element_type=jnp.float32)
    mixed = (
        mixed
        + own_share.astype(jnp.float32)[..., None] * fresh_values.astype(jnp.float32)[:, :, None, :]
    )
    return mixed


def split_kernel(grid, place_ref, rows_ref, *out_refs):
    squares_ref = out_refs[-1]
    step = pl.program_id(0)
    low = place_ref[0]
    block = rows_ref[...]
    wide = block.astype(jnp.float32)

    @pl.when(step == 0)
    def _():
        squares_ref[...] = jnp.zeros_like(squares_ref)

    part = (wide * wide)[:, :LANES]
    for at in range(LANES, wide.shape[1], LANES):
        span = wide[:, at : at + LANES]
        part = part + span * span
    squares_ref[...] += part
    for dg in range(grid.pair):
        half = lax.rem(low + dg, grid.pair)
        start = pl.multiple_of(half * grid.sub, LANES)
        out_refs[dg][...] = rows_ref[:, pl.ds(start, grid.sub)]


def split(grid, rows, low, y_there):
    span_rows, width = rows.shape
    shard = grid.sub * grid.pair
    steps = grid.zs * CORES
    place = jnp.stack([low, y_there]).astype(jnp.int32)

    def column(step, place_ref):
        return (0, ((step // CORES) * grid.ys + place_ref[1]) * CORES + step % CORES)

    piece = jax.ShapeDtypeStruct((span_rows, steps * grid.sub), rows.dtype)
    return pl.pallas_call(
        functools.partial(split_kernel, grid),
        grid_spec=pltpu.PrefetchScalarGridSpec(
            num_scalar_prefetch=1,
            grid=(steps,),
            in_specs=[pl.BlockSpec((span_rows, shard), column)],
            out_specs=[
                pl.BlockSpec((span_rows, grid.sub), lambda step, place_ref: (0, step))
                for _ in range(grid.pair)
            ]
            + [pl.BlockSpec((span_rows, LANES), lambda step, place_ref: (0, 0))],
        ),
        out_shape=[piece] * grid.pair
        + [jax.ShapeDtypeStruct((span_rows, LANES), jnp.float32)],
        name="split",
    )(place, rows)


def product_kernel(grid, order, blocks, place_ref, *refs):
    pieces = len(order)
    acts = refs[:blocks]
    weights = refs[blocks : blocks + pieces]
    outs = refs[blocks + pieces : 2 * blocks + pieces]
    act_store, weight_store, act_sems, weight_sems = refs[2 * blocks + pieces :]
    rows = acts[0].shape[0]
    act_copies = [
        pltpu.make_async_copy(acts[at], act_store.at[pl.ds(at * rows, rows)], act_sems.at[at])
        for at in range(blocks)
    ]
    weight_copies = [
        pltpu.make_async_copy(weights[at], weight_store.at[at], weight_sems.at[at])
        for at in range(pieces)
    ]
    weight_copies[0].start()
    for copy in act_copies:
        copy.start()
    for copy in weight_copies[1:]:
        copy.start()
    for copy in act_copies:
        copy.wait()
    total = None
    for at, (dz, dc) in enumerate(order):
        weight_copies[at].wait()
        z_there = lax.rem(place_ref[0] + grid.zs - dz, grid.zs)
        c_there = lax.rem(place_ref[1] + CORES - dc, CORES)
        start = pl.multiple_of((z_there * CORES + c_there) * grid.sub, LANES)
        term = jnp.dot(
            act_store[:, pl.ds(start, grid.sub)],
            weight_store[at],
            preferred_element_type=jnp.float32,
        )
        total = term if total is None else total + term
    for at in range(blocks):
        outs[at][...] = total[at * rows : (at + 1) * rows].astype(outs[at].dtype)


def product(grid, acts, weights, order, z, c):
    blocks, pieces = len(acts), len(weights)
    rows, depth = acts[0].shape
    width = weights[0].shape[1]
    place = jnp.stack([z, c]).astype(jnp.int32)
    kinds = [jnp.float32] + [jnp.bfloat16] * (blocks - 1)
    anywhere = pl.BlockSpec(memory_space=pl.ANY)
    inside = pl.BlockSpec(memory_space=pltpu.VMEM)
    return pl.pallas_call(
        functools.partial(product_kernel, grid, order, blocks),
        in_specs=[pl.BlockSpec(memory_space=pltpu.SMEM)] + [anywhere] * (blocks + pieces),
        out_specs=[inside] * blocks,
        out_shape=[jax.ShapeDtypeStruct((rows, width), kind) for kind in kinds],
        scratch_shapes=[
            pltpu.VMEM((blocks * rows, depth), acts[0].dtype),
            pltpu.VMEM((pieces,) + weights[0].shape, weights[0].dtype),
            pltpu.SemaphoreType.DMA((blocks,)),
            pltpu.SemaphoreType.DMA((pieces,)),
        ],
        name="product",
    )(place, *acts, *weights)


def per_device(
    grid,
    prompt_rows,
    decode_rows,
    norm_gain,
    w_query,
    w_key,
    w_value,
    key_cache,
    value_cache,
    positions,
    lengths,
    slots,
):
    span_rows, width = prompt_rows.shape
    shard_rows, key_columns = w_key.shape
    kv_heads, head_size = key_cache.shape[1], key_cache.shape[3]
    own_rows = decode_rows.shape[0]
    low = lax.rem(lax.axis_index("grp"), grid.pair)
    me = lax.axis_index("gx")
    z = me // (grid.ys * CORES)
    y = lax.rem(me // CORES, grid.ys)
    c = lax.rem(me, CORES)

    acts, squares = [], None
    for dy in range(grid.ys):
        outs = split(grid, prompt_rows, low, lax.rem(y + dy, grid.ys))
        squares = outs[-1] if squares is None else squares + outs[-1]
        for dg in range(grid.pair):
            acts.append(outs[dg] if dg + dy == 0 else grid.send(outs[dg], dg=dg, dy=dy))

    rows_here = jnp.concatenate([decode_rows, prompt_rows[span_rows - 1 :]], axis=0)
    kinds = own_rows + 1
    normed = normalize(rows_here, norm_gain).reshape(kinds, width // LANES, LANES)
    along_z = jnp.concatenate(
        [normed] + [grid.send(normed, dz=dz) for dz in range(1, grid.zs)], axis=0
    )
    plane = jnp.concatenate(
        [along_z] + [grid.send(along_z, dy=dy) for dy in range(1, grid.ys)], axis=0
    )
    every = jnp.concatenate([plane, grid.send(plane, dc=1)], axis=0)
    every = every.reshape(every.shape[0], width)

    gain_here = lax.dynamic_slice_in_dim(norm_gain, me * shard_rows + low * grid.sub, grid.sub, 0)
    piece = lax.dynamic_slice_in_dim(w_key, low * grid.sub, grid.sub, 0)
    piece = (piece.astype(jnp.float32) * gain_here.astype(jnp.float32)[:, None]).astype(w_key.dtype)
    order, pieces = [], []
    for dz in range(grid.zs):
        here = piece if dz == 0 else grid.send(piece, dz=dz)
        order += [(dz, 0), (dz, 1)]
        pieces += [here, grid.send(here, dc=1)]

    row_ids = jnp.arange(lengths.shape[0], dtype=jnp.int32)
    hit = slots[None, :] == row_ids[:, None]
    span_of = jnp.sum(jnp.where(hit, jnp.arange(slots.shape[0], dtype=jnp.int32)[None, :], 0), axis=1)
    taken = jnp.any(hit, axis=1)
    source = jnp.where(taken, span_of, row_ids // own_rows)
    inner = jnp.where(taken, own_rows, row_ids % own_rows)
    from_c = lax.rem(c - source % CORES + CORES, CORES)
    from_y = lax.rem(y - (source // CORES) % grid.ys + grid.ys, grid.ys)
    from_z = lax.rem(z - source // (CORES * grid.ys) + grid.zs, grid.zs)
    at = ((from_c * grid.ys + from_y) * grid.zs + from_z) * kinds + inner
    pick = (at[:, None] == jnp.arange(every.shape[0], dtype=jnp.int32)[None, :]).astype(jnp.float32)

    query_cos, query_sin = angles_of(lengths, head_size)
    query_sums = jnp.dot(every, w_query, preferred_element_type=jnp.float32)
    query_sums = jnp.dot(pick, query_sums, precision=lax.Precision.HIGHEST)
    total_rows = query_sums.shape[0]
    queries = rotate(query_sums.reshape(total_rows, -1, head_size), query_cos, query_sin)
    queries = queries.reshape(total_rows, -1).astype(jnp.bfloat16)
    features = lax.dynamic_slice_in_dim(every, me * shard_rows, shard_rows, 1)
    fresh = jnp.concatenate(
        [
            jnp.dot(features, w_key, preferred_element_type=jnp.float32),
            jnp.dot(features, w_value, preferred_element_type=jnp.float32),
        ],
        axis=1,
    )
    fresh = jnp.dot(pick, fresh, precision=lax.Precision.HIGHEST).astype(jnp.bfloat16)
    query_columns = queries.shape[1]
    packet = jnp.concatenate([queries, fresh], axis=1).reshape(grid.count, own_rows, -1)
    packet = lax.all_to_all(packet, "gx", split_axis=0, concat_axis=0)

    own_queries = packet[:, :, :query_columns].transpose(1, 0, 2).reshape(own_rows, -1)
    fresh = jnp.sum(packet[:, :, query_columns:].astype(jnp.float32), axis=0)
    own_lengths = lax.dynamic_slice_in_dim(lengths, me * own_rows, own_rows, 0)
    own_cos, own_sin = angles_of(own_lengths, head_size)
    new_keys = rotate(
        fresh[:, :key_columns].reshape(own_rows, kv_heads, head_size), own_cos, own_sin
    ).astype(jnp.bfloat16)
    new_values = fresh[:, key_columns:].reshape(own_rows, kv_heads, head_size).astype(jnp.bfloat16)
    all_heads = own_queries.shape[1] // head_size
    grouped = own_queries.reshape(own_rows, kv_heads, all_heads // kv_heads, head_size)
    mixed = attend(grouped, key_cache, value_cache, new_keys, new_values, own_lengths)
    attended = mixed.reshape(own_rows, all_heads * head_size).astype(jnp.bfloat16)

    partial = product(grid, acts, pieces, order, z, c)
    key_sums = partial[0]
    at = 0
    for dy in range(grid.ys):
        for dg in range(grid.pair):
            if at:
                key_sums = key_sums + grid.send(partial[at], dg=-dg, dy=-dy).astype(jnp.float32)
            at += 1
    square_mean = jnp.sum(squares, axis=1, keepdims=True) / width
    key_sums = key_sums * lax.rsqrt(square_mean + EPSILON)
    cosine, sine = angles_of(positions, head_size)
    prompt_keys = rotate(key_sums.reshape(span_rows, kv_heads, head_size), cosine, sine)
    prompt_keys = prompt_keys.reshape(span_rows, key_columns).astype(jnp.bfloat16)
    return (prompt_keys, attended)


def solution(mesh):
    def run(*args):
        shard_rows = args[4].shape[0] // mesh.shape["gx"]
        grid = Grid(mesh, shard_rows)
        return jax.shard_map(
            functools.partial(per_device, grid),
            mesh=mesh,
            in_specs=(
                P(("grp", "gx"), None),
                P(("grp", "gx"), None),
                P(),
                P(None, "gx"),
                P("gx", None),
                P("gx", None),
                P(("grp", "gx"), None, None, None),
                P(("grp", "gx"), None, None, None),
                P(("grp", "gx")),
                P("grp"),
                P("grp"),
            ),
            out_specs=(P(("grp", "gx"), None), P(("grp", "gx"), None)),
            check_vma=False,
        )(*args)

    return run
```

time: 294 us -> 141 us (0.48)
  waiting for transfers between devices: 204 us -> 32.2 us
  starting transfers between devices: 3.76 us -> 34.3 us
  blocking collectives: 27.9 us -> 0 us
  Pallas kernels: 0 us -> 20.6 us
  between operations: 14.7 us -> 1.2 us
  local copies, waits for them, and re-layouts: 10.2 us -> 21.5 us
  matrix products: 19.5 us -> 11.7 us
  other arithmetic: 13.2 us -> 18.5 us
    all_gather x2 -> x0, waiting for transfers between devices: 133 us -> none  [the longest x1 127 us: per_device(): lax.all_gather(w_key, 'gx', axis=0, tiled=True)]
    unnamed x4 -> x0, waiting for transfers between devices: 66.2 us -> none
    all_gather x1 -> x0, blocking collectives: 27.9 us -> none  [per_device(): finals = lax.all_gather(final_row, 'gx', axis=0, tiled=True)]
    ppermute x0 -> x18, waiting for transfers between devices: none -> 25.6 us  [send(): return lax.ppermute(value, BOTH, self.perm(**offsets))]
    pallas_call x0 -> x3, Pallas kernels: none -> 20.6 us  [the longest x2 13.1 us: split(): pl.pallas_call(functools.partial(split_kernel, grid), grid_spec=pltpu.Pre...]
    ppermute x0 -> x18, starting transfers between devices: none -> 20.5 us  [send(): return lax.ppermute(value, BOTH, self.perm(**offsets))]
    concatenate x0 -> x2, local copies, waits for them, and re-layouts: none -> 12.3 us  [the longest x1 11.5 us: per_device(): every = jnp.concatenate([plane, grid.send(plane, dc=1)], axis=0)]
    all_to_all x1, starting transfers between devices: 3.63 us -> 13.9 us  [per_device(): packet = lax.all_to_all(packet, 'gx', split_axis=0, concat_axis=0)]
  transfers between devices with their start and end apart: 4 -> 19, of which waited for: 4 -> 6; matrix products, arithmetic and copies ran while one was open for 7% -> 17% of each run, Pallas kernels for 0% -> 15%
where the time goes in v1:
time: 141 us; the launch traced here: 140 us
  starting transfers between devices  34.3 us (24%)
  waiting for transfers between devices  32.2 us (23%)
  local copies, waits for them, and re-layouts  21.5 us (15%)
  Pallas kernels  20.6 us (15%)
  other arithmetic  18.5 us (13%)
  matrix products  11.7 us (8%)
    ppermute x18, waiting for transfers between devices, send(): return lax.ppermute(value, BOTH, self.perm(**offsets))  25.6 us
    ppermute x18, starting transfers between devices, send(): return lax.ppermute(value, BOTH, self.perm(**offsets))  20.5 us
    all_to_all x1, starting transfers between devices, per_device(): packet = lax.all_to_all(packet, 'gx', split_axis=0, concat_axis=0)  13.9 us
    pallas_call x2, Pallas kernels, split(): pl.pallas_call(functools.partial(split_kernel, grid), grid_spec=pltpu.Pre...  13.1 us
    concatenate x1, local copies, waits for them, and re-layouts, per_device(): every = jnp.concatenate([plane, grid.send(plane, dc=1)], axis=0)  11.5 us
    dot_general x1, matrix products, per_device(): query_sums = jnp.dot(every, w_query, preferred_element_type=jnp.float32)  8.72 us
    pallas_call x1, Pallas kernels, product(): pl.pallas_call(functools.partial(product_kernel, grid, order, blocks), in...  7.48 us
    unnamed x67, local copies, waits for them, and re-layouts  6.71 us
  transfers between devices with their start and end apart: 19, of which 6 were waited for; matrix products, arithmetic and copies ran while one was open for 17% of the time, Pallas kernels for 15%

profile of v1, /device:TPU:0, one launch (start us, length us, event | category | flops | bytes accessed | tf_op | source)
XLA Modules:
  0.0 140.0 jit_solution(6076312631494486999)
XLA Ops:
  0.7 0.8 dynamic-slice_convert_fusion
  1.5 1.2 multiply_convert_fusion.refs_4_
  2.7 0.6 collective-permute-start.3
  3.3 2.6 %collective-permute-start.4 = (bf16[512,512]{1,0:T(8,128)(2,1)S(1)}, bf16[512,512]{1,0:T(8,128)(2,1)}, u32[]{:S(2)}, u32[]{:S(2)}) collective-permute-start(bf16[512,512]{1,0:T(8,128)(2,1)S(1)} %multiply_convert_fusion.refs_4_), channel_id=1, source_target_pairs={{0,4},{1,5},{2,6},{3,7},{4,8},{5,9},{6,10},{7,11},{8,12},{9,13},{1... | collective-permute-start | bytes 1572872 | tf_op jit(solution)/shard_map/ppermute | solution.py:47
  5.9 0.6 pad_add_fusion.1
  6.5 6.5 %split.2 = (bf16[128,4096]{1,0:T(8,128)(2,1)}, bf16[128,4096]{1,0:T(8,128)(2,1)}, f32[128,128]{1,0:T(8,128)}) custom-call(s32[2]{0:T(128)} %get-tuple-element.49.place_ref, bf16[128,16384]{1,0:T(8,128)(2,1)} %rows_ref.3), custom_call_target="tpu_custom_call" | custom-call | tf_op jit(solution)/shard_map/split/pallas_call | solution.py:127
  13.0 1.5 %collective-permute-start = (bf16[128,4096]{1,0:T(8,128)(2,1)}, bf16[128,4096]{1,0:T(8,128)(2,1)S(1)}, u32[]{:S(2)}, u32[]{:S(2)}) collective-permute-start(bf16[128,4096]{1,0:T(8,128)(2,1)} %get-tuple-element.13), channel_id=1, source_target_pairs={{0,16},{1,17},{2,18},{3,19},{4,20},{5,21},{6,22},{7,23},{8,24},{9,... | collective-permute-start | bytes 3145736 | tf_op jit(solution)/shard_map/ppermute | solution.py:47
  14.5 6.6 %split.3 = (bf16[128,4096]{1,0:T(8,128)(2,1)}, bf16[128,4096]{1,0:T(8,128)(2,1)}, f32[128,128]{1,0:T(8,128)}) custom-call(s32[2]{0:T(128)} %get-tuple-element.50.place_ref, bf16[128,16384]{1,0:T(8,128)(2,1)} %rows_ref.3), custom_call_target="tpu_custom_call" | custom-call | tf_op jit(solution)/shard_map/split/pallas_call | solution.py:127
  21.2 1.6 %collective-permute-start.1 = (bf16[128,4096]{1,0:T(8,128)(2,1)}, bf16[128,4096]{1,0:T(8,128)(2,1)}, u32[]{:S(2)}, u32[]{:S(2)}) collective-permute-start(bf16[128,4096]{1,0:T(8,128)(2,1)} %get-tuple-element.14), channel_id=1, source_target_pairs={{0,2},{1,3},{2,0},{3,1},{4,6},{5,7},{6,4},{7,5},{8,10},{9,11},{10,... | collective-permute-start | bytes 3145736 | tf_op jit(solution)/shard_map/ppermute | solution.py:47
  22.8 1.2 slice_reduce_fusion
  23.9 0.3 fusion.3
  24.3 0.7 constant_dynamic-update-slice_fusion.4
  25.0 1.6 %collective-permute-start.13 = (bf16[3,128,128]{2,1,0:T(8,128)(2,1)S(1)}, bf16[3,128,128]{2,1,0:T(8,128)(2,1)S(1)}, u32[]{:S(2)}, u32[]{:S(2)}) collective-permute-start(bf16[3,128,128]{2,1,0:T(8,128)(2,1)S(1)} %get-tuple-element.25), channel_id=1, source_target_pairs={{0,4},{1,5},{2,6},{3,7},{4,8},{5,9},{6,10},{7,11},{8,12},{9,13},{1... | collective-permute-start | bytes 294920 | tf_op jit(solution)/shard_map/ppermute | solution.py:47
  26.6 0.9 fusion.5
  27.5 0.3 multiply_cosine_fusion
  27.8 0.8 multiply_cosine_fusion.1
  28.5 0.6 fusion.48
  29.2 0.6 iota_compare_fusion.4
  29.8 1.0 add_reduce_fusion
  30.8 0.5 add_rsqrt_fusion.1
  31.3 0.8 pad_maximum_fusion.3
  32.0 1.2 collective-permute-start.14
  33.3 0.6 fusion.20
  33.8 5.2 %collective-permute-done.14 = bf16[3,128,128]{2,1,0:T(8,128)(2,1)S(1)} collective-permute-done((bf16[3,128,128]{2,1,0:T(8,128)(2,1)S(1)}, bf16[3,128,128]{2,1,0:T(8,128)(2,1)S(1)}, u32[]{:S(2)}, u32[]{:S(2)}) %collective-permute-start.14) | collective-permute-done | bytes 98336 | tf_op jit(solution)/shard_map/ppermute | solution.py:47
  39.1 2.2 %collective-permute-start.15 = (bf16[3,128,128]{2,1,0:T(8,128)(2,1)S(1)}, bf16[3,128,128]{2,1,0:T(8,128)(2,1)S(1)}, u32[]{:S(2)}, u32[]{:S(2)}) collective-permute-start(bf16[3,128,128]{2,1,0:T(8,128)(2,1)S(1)} %get-tuple-element.25), channel_id=1, source_target_pairs={{0,12},{1,13},{2,14},{3,15},{4,0},{5,1},{6,2},{7,3},{8,4},{9,5},{1... | collective-permute-start | bytes 294920 | tf_op jit(solution)/shard_map/ppermute | solution.py:47
  41.3 0.6 select_reduce_fusion
  41.9 1.8 %collective-permute-done.15 = bf16[3,128,128]{2,1,0:T(8,128)(2,1)S(1)} collective-permute-done((bf16[3,128,128]{2,1,0:T(8,128)(2,1)S(1)}, bf16[3,128,128]{2,1,0:T(8,128)(2,1)S(1)}, u32[]{:S(2)}, u32[]{:S(2)}) %collective-permute-start.15) | collective-permute-done | bytes 98336 | tf_op jit(solution)/shard_map/ppermute | solution.py:47
  43.7 0.7 collective-permute-start.6
  44.4 3.3 %collective-permute-start.8 = (bf16[512,512]{1,0:T(8,128)(2,1)S(1)}, bf16[512,512]{1,0:T(8,128)(2,1)}, u32[]{:S(2)}, u32[]{:S(2)}) collective-permute-start(bf16[512,512]{1,0:T(8,128)(2,1)S(1)} %multiply_convert_fusion.refs_4_), channel_id=1, source_target_pairs={{0,12},{1,13},{2,14},{3,15},{4,0},{5,1},{6,2},{7,3},{8,4},{9,5},{1... | collective-permute-start | bytes 1572872 | tf_op jit(solution)/shard_map/ppermute | solution.py:47
  47.8 0.5 collective-permute-start.2
  48.2 1.5 %pad_maximum_fusion.5 = (f32[32,128]{1,0:T(8,128)S(1)}, f32[32,128]{1,0:T(8,128)}) fusion(f32[32,64]{1,0:T(8,128)} %get-tuple-element.41, f32[32,64]{1,0:T(8,128)} %get-tuple-element.43, f32[32,64]{1,0:T(8,128)} %get-tuple-element.42), kind=kLoop, calls=%fused_computation.50 | loop fusion | flops 8192 | bytes 57344 | tf_op jit(solution)/shard_map/concatenate | solution.py:62
  49.7 1.2 fusion.31
  50.9 1.3 multiply_cosine_fusion.2
  52.3 17.5 %collective-permute-done.6.refs_8_ = bf16[512,512]{1,0:T(8,128)(2,1)} collective-permute-done((bf16[512,512]{1,0:T(8,128)(2,1)S(1)}, bf16[512,512]{1,0:T(8,128)(2,1)}, u32[]{:S(2)}, u32[]{:S(2)}) %collective-permute-start.6) | collective-permute-done | bytes 524320 | tf_op jit(solution)/shard_map/ppermute | solution.py:47
  69.7 0.5 collective-permute-start.7
  70.3 0.9 pad_maximum_fusion
  71.2 0.5 collective-permute-start.16
  71.7 0.7 pad_add_fusion.place_ref
  72.4 0.6 constant_dynamic-update-slice_fusion.3
  73.0 0.7 constant_dynamic-update-slice_fusion.2
  73.7 0.6 constant_dynamic-update-slice_fusion.1
  74.4 7.5 %product.1 = (f32[128,512]{1,0:T(8,128)}, bf16[128,512]{1,0:T(8,128)(2,1)}, bf16[128,512]{1,0:T(8,128)(2,1)}, bf16[128,512]{1,0:T(8,128)(2,1)}) custom-call(s32[2]{0:T(128)} %pad_add_fusion.place_ref, bf16[128,4096]{1,0:T(8,128)(2,1)} %get-tuple-element.12.refs_0_, bf16[128,4096]{1,0:T(8,128)(2,1)} %copy-done.4, ...), custom_call_target="tpu_custom_call" | custom-call | tf_op jit(solution)/shard_map/product/pallas_call | solution.py:191
  81.9 1.6 %collective-permute-start.12 = (bf16[128,512]{1,0:T(8,128)(2,1)}, bf16[128,512]{1,0:T(8,128)(2,1)S(1)}, u32[]{:S(2)}, u32[]{:S(2)}) collective-permute-start(bf16[128,512]{1,0:T(8,128)(2,1)} %get-tuple-element.19), channel_id=1, source_target_pairs={{0,18},{1,19},{2,16},{3,17},{4,22},{5,23},{6,20},{7,21},{8,26},{9,... | collective-permute-start | bytes 393224 | tf_op jit(solution)/shard_map/ppermute | solution.py:47
  83.4 0.7 collective-permute-start.11
  84.1 1.3 collective-permute-start.10
  85.4 0.8 constant_dynamic-update-slice_fusion
  86.2 0.7 pad_maximum_fusion.7
  86.9 0.7 copy.43
  87.6 0.8 copy.42
  88.4 0.8 copy.41
  89.2 1.1 copy.23
  90.4 1.0 collective-permute-done.11
  91.8 0.9 maximum_multiply_fusion
  92.8 0.5 copy.40
  93.3 11.5 %concatenate.80 = bf16[48,16384]{1,0:T(8,128)(2,1)S(1)} concatenate(bf16[3,16384]{1,0:T(4,128)(2,1)S(1)} %copy-done.9, bf16[3,16384]{1,0:T(4,128)(2,1)} %bitcast.81, bf16[3,16384]{1,0:T(4,128)(2,1)} %bitcast.82, bf16[3,16384]{1,0:T(4,128)(2,1)} %bitcast.83, bf16[12,16384]{1,0:T(8,128)(2,1)} %bitcast.73, bf16[24,16384]{1,0:T(8,128)(2,1)S(1)} %bitcast.71), dimensions={0} | concatenate | bytes 3145728 | tf_op jit(solution)/shard_map/concatenate | solution.py:246
  104.8 1.5 %fusion.12 = f32[48,512]{1,0:T(8,128)S(1)} fusion(bf16[1024,512]{1,0:T(8,128)(2,1)} %param.15, bf16[48,16384]{1,0:T(8,128)(2,1)S(1)} %concatenate.80, s32[]{:T(128)S(6)} %select_n.106), kind=kOutput, calls=%fused_computation.34 | convolution fusion | flops 50331648 | bytes 1245188 | tf_op jit(solution)/shard_map/dot_general | solution.py:279
  106.3 0.3 fusion.10
  106.6 8.7 %fusion.53 = f32[48,512]{1,0:T(8,128)S(1)} fusion(bf16[48,16384]{1,0:T(8,128)(2,1)S(1)} %concatenate.80, bf16[16384,512]{1,0:T(8,128)(2,1)} %param.14), kind=kOutput, calls=%fused_computation.136 | convolution fusion | flops 805306368 | bytes 18448384 | tf_op jit(solution)/shard_map/dot_general | solution.py:271
  116.3 0.7 reshape.225
  116.9 13.9 %all-to-all-start = ((bf16[16,2,1536]{2,1,0:T(2,128)(2,1)}), bf16[16,2,1536]{2,1,0:T(2,128)(2,1)S(1)}, u32[]{:S(2)}, u32[]{:S(2)}) async-start(bf16[16,2,1536]{2,1,0:T(2,128)(2,1)} %reshape.225), calls=%async_computation | async-start | bytes 196608 | tf_op jit(solution)/shard_map/all_to_all | solution.py:287
  130.9 0.7 fusion.6
  131.6 6.6 %all-to-all-done = bf16[16,2,1536]{2,1,0:T(2,128)(2,1)S(1)} async-done(((bf16[16,2,1536]{2,1,0:T(2,128)(2,1)}), bf16[16,2,1536]{2,1,0:T(2,128)(2,1)S(1)}, u32[]{:S(2)}, u32[]{:S(2)}) %all-to-all-start) | async-done | bytes 98336 | tf_op jit(solution)/shard_map/all_to_all | solution.py:287
  138.7 0.3 fusion.52
  139.3 0.7 copy.45
  (105 shorter events, 2.3 us)
Async XLA Ops:
  0.6 105.7 %copy-start = (bf16[1024,512]{1,0:T(8,128)(2,1)S(1)}, bf16[1024,512]{1,0:T(8,128)(2,1)}, u32[]{:S(2)}) copy-start(bf16[1024,512]{1,0:T(8,128)(2,1)} %param.16) | copy-start | bytes 3145732
  2.7 41.7 %copy-start.3 = (bf16[512,512]{1,0:T(8,128)(2,1)}, bf16[512,512]{1,0:T(8,128)(2,1)S(1)}, u32[]{:S(2)}) copy-start(bf16[512,512]{1,0:T(8,128)(2,1)S(1)} %multiply_convert_fusion.refs_4_) | copy-start | bytes 1572868
  2.7 41.7 %collective-permute-start.3 = (bf16[512,512]{1,0:T(8,128)(2,1)S(1)}, bf16[512,512]{1,0:T(8,128)(2,1)S(1)}, u32[]{:S(2)}, u32[]{:S(2)}) collective-permute-start(bf16[512,512]{1,0:T(8,128)(2,1)S(1)} %multiply_convert_fusion.refs_4_), channel_id=1, source_target_pairs={{0,1},{1,0},{2,3},{3,2},{4,5},{5,4},{6,7},{7,6},{8,9},{9,8},{10,11... | collective-permute-start | bytes 1572872 | tf_op jit(solution)/shard_map/ppermute | solution.py:47
  3.3 44.5 %collective-permute-start.4 = (bf16[512,512]{1,0:T(8,128)(2,1)S(1)}, bf16[512,512]{1,0:T(8,128)(2,1)}, u32[]{:S(2)}, u32[]{:S(2)}) collective-permute-start(bf16[512,512]{1,0:T(8,128)(2,1)S(1)} %multiply_convert_fusion.refs_4_), channel_id=1, source_target_pairs={{0,4},{1,5},{2,6},{3,7},{4,8},{5,9},{6,10},{7,11},{8,12},{9,13},{1... | collective-permute-start | bytes 1572872 | tf_op jit(solution)/shard_map/ppermute | solution.py:47
  13.0 57.2 %collective-permute-start = (bf16[128,4096]{1,0:T(8,128)(2,1)}, bf16[128,4096]{1,0:T(8,128)(2,1)S(1)}, u32[]{:S(2)}, u32[]{:S(2)}) collective-permute-start(bf16[128,4096]{1,0:T(8,128)(2,1)} %get-tuple-element.13), channel_id=1, source_target_pairs={{0,16},{1,17},{2,18},{3,19},{4,20},{5,21},{6,22},{7,23},{8,24},{9,... | collective-permute-start | bytes 3145736 | tf_op jit(solution)/shard_map/ppermute | solution.py:47
  14.5 8.2 %copy-start.14 = (bf16[16384]{0:T(1024)(128)(2,1)S(1)}, bf16[16384]{0:T(1024)(128)(2,1)}, u32[]{:S(2)}) copy-start(bf16[16384]{0:T(1024)(128)(2,1)} %param.13) | copy-start | bytes 98308
  14.5 9.4 %copy-start.6 = (bf16[2,16384]{1,0:T(2,128)(2,1)S(1)}, bf16[2,16384]{1,0:T(2,128)(2,1)}, u32[]{:S(2)}) copy-start(bf16[2,16384]{1,0:T(2,128)(2,1)} %param.12) | copy-start | bytes 196612
  14.5 12.1 %copy-start.26 = (s32[128]{0:T(128)S(1)}, s32[128]{0:T(128)}, u32[]{:S(2)}) copy-start(s32[128]{0:T(128)} %param.19) | copy-start | bytes 1540
  14.5 12.9 %copy-start.24 = (s32[32]{0:T(128)S(1)}, s32[32]{0:T(128)}, u32[]{:S(2)}) copy-start(s32[32]{0:T(128)} %param.20) | copy-start | bytes 388
  21.2 12.1 %copy-start.27 = (s32[16]{0:T(128)S(1)}, s32[16]{0:T(128)}, u32[]{:S(2)}) copy-start(s32[16]{0:T(128)} %param.21) | copy-start | bytes 196
  21.2 50.1 %collective-permute-start.1 = (bf16[128,4096]{1,0:T(8,128)(2,1)}, bf16[128,4096]{1,0:T(8,128)(2,1)}, u32[]{:S(2)}, u32[]{:S(2)}) collective-permute-start(bf16[128,4096]{1,0:T(8,128)(2,1)} %get-tuple-element.14), channel_id=1, source_target_pairs={{0,2},{1,3},{2,0},{3,1},{4,6},{5,7},{6,4},{7,5},{8,10},{9,11},{10,... | collective-permute-start | bytes 3145736 | tf_op jit(solution)/shard_map/ppermute | solution.py:47
  25.0 7.0 %collective-permute-start.13 = (bf16[3,128,128]{2,1,0:T(8,128)(2,1)S(1)}, bf16[3,128,128]{2,1,0:T(8,128)(2,1)S(1)}, u32[]{:S(2)}, u32[]{:S(2)}) collective-permute-start(bf16[3,128,128]{2,1,0:T(8,128)(2,1)S(1)} %get-tuple-element.25), channel_id=1, source_target_pairs={{0,4},{1,5},{2,6},{3,7},{4,8},{5,9},{6,10},{7,11},{8,12},{9,13},{1... | collective-permute-start | bytes 294920 | tf_op jit(solution)/shard_map/ppermute | solution.py:47
  26.6 1.2 copy-start.16
  32.0 7.0 %collective-permute-start.14 = (bf16[3,128,128]{2,1,0:T(8,128)(2,1)S(1)}, bf16[3,128,128]{2,1,0:T(8,128)(2,1)S(1)}, u32[]{:S(2)}, u32[]{:S(2)}) collective-permute-start(bf16[3,128,128]{2,1,0:T(8,128)(2,1)S(1)} %get-tuple-element.25), channel_id=1, source_target_pairs={{0,8},{1,9},{2,10},{3,11},{4,12},{5,13},{6,14},{7,15},{8,0},{9,1},... | collective-permute-start | bytes 294920 | tf_op jit(solution)/shard_map/ppermute | solution.py:47
  39.1 4.6 %collective-permute-start.15 = (bf16[3,128,128]{2,1,0:T(8,128)(2,1)S(1)}, bf16[3,128,128]{2,1,0:T(8,128)(2,1)S(1)}, u32[]{:S(2)}, u32[]{:S(2)}) collective-permute-start(bf16[3,128,128]{2,1,0:T(8,128)(2,1)S(1)} %get-tuple-element.25), channel_id=1, source_target_pairs={{0,12},{1,13},{2,14},{3,15},{4,0},{5,1},{6,2},{7,3},{8,4},{9,5},{1... | collective-permute-start | bytes 294920 | tf_op jit(solution)/shard_map/ppermute | solution.py:47
  43.7 26.0 %collective-permute-start.6 = (bf16[512,512]{1,0:T(8,128)(2,1)S(1)}, bf16[512,512]{1,0:T(8,128)(2,1)}, u32[]{:S(2)}, u32[]{:S(2)}) collective-permute-start(bf16[512,512]{1,0:T(8,128)(2,1)S(1)} %multiply_convert_fusion.refs_4_), channel_id=1, source_target_pairs={{0,8},{1,9},{2,10},{3,11},{4,12},{5,13},{6,14},{7,15},{8,0},{9,1},... | collective-permute-start | bytes 1572872 | tf_op jit(solution)/shard_map/ppermute | solution.py:47
  44.4 29.9 %copy-start.7 = (bf16[512,512]{1,0:T(8,128)(2,1)}, bf16[512,512]{1,0:T(8,128)(2,1)S(1)}, u32[]{:S(2)}) copy-start(bf16[512,512]{1,0:T(8,128)(2,1)S(1)} %collective-permute-done.3.refs_5_) | copy-start | bytes 1572868
  44.4 25.3 %collective-permute-start.8 = (bf16[512,512]{1,0:T(8,128)(2,1)S(1)}, bf16[512,512]{1,0:T(8,128)(2,1)}, u32[]{:S(2)}, u32[]{:S(2)}) collective-permute-start(bf16[512,512]{1,0:T(8,128)(2,1)S(1)} %multiply_convert_fusion.refs_4_), channel_id=1, source_target_pairs={{0,12},{1,13},{2,14},{3,15},{4,0},{5,1},{6,2},{7,3},{8,4},{9,5},{1... | collective-permute-start | bytes 1572872 | tf_op jit(solution)/shard_map/ppermute | solution.py:47
  47.8 26.6 %collective-permute-start.2 = (bf16[128,4096]{1,0:T(8,128)(2,1)}, bf16[128,4096]{1,0:T(8,128)(2,1)}, u32[]{:S(2)}, u32[]{:S(2)}) collective-permute-start(bf16[128,4096]{1,0:T(8,128)(2,1)} %get-tuple-element.15), channel_id=1, source_target_pairs={{0,18},{1,19},{2,16},{3,17},{4,22},{5,23},{6,20},{7,21},{8,26},{9,... | collective-permute-start | bytes 3145736 | tf_op jit(solution)/shard_map/ppermute | solution.py:47
  69.7 4.6 %collective-permute-start.5 = (bf16[512,512]{1,0:T(8,128)(2,1)}, bf16[512,512]{1,0:T(8,128)(2,1)}, u32[]{:S(2)}, u32[]{:S(2)}) collective-permute-start(bf16[512,512]{1,0:T(8,128)(2,1)} %collective-permute-done.4.refs_6_), channel_id=1, source_target_pairs={{0,1},{1,0},{2,3},{3,2},{4,5},{5,4},{6,7},{7,6},{8,9},{9,8},{10,11... | collective-permute-start | bytes 1572872 | tf_op jit(solution)/shard_map/ppermute | solution.py:47
  69.7 4.6 %collective-permute-start.7 = (bf16[512,512]{1,0:T(8,128)(2,1)}, bf16[512,512]{1,0:T(8,128)(2,1)}, u32[]{:S(2)}, u32[]{:S(2)}) collective-permute-start(bf16[512,512]{1,0:T(8,128)(2,1)} %collective-permute-done.6.refs_8_), channel_id=1, source_target_pairs={{0,1},{1,0},{2,3},{3,2},{4,5},{5,4},{6,7},{7,6},{8,9},{9,8},{10,11... | collective-permute-start | bytes 1572872 | tf_op jit(solution)/shard_map/ppermute | solution.py:47
  70.2 4.1 %copy-start.4 = (bf16[128,4096]{1,0:T(8,128)(2,1)}, bf16[128,4096]{1,0:T(8,128)(2,1)S(1)}, u32[]{:S(2)}) copy-start(bf16[128,4096]{1,0:T(8,128)(2,1)S(1)} %collective-permute-done.refs_1_) | copy-start | bytes 3145732
  70.2 4.1 %collective-permute-start.9 = (bf16[512,512]{1,0:T(8,128)(2,1)}, bf16[512,512]{1,0:T(8,128)(2,1)}, u32[]{:S(2)}, u32[]{:S(2)}) collective-permute-start(bf16[512,512]{1,0:T(8,128)(2,1)} %collective-permute-done.8.refs_10_), channel_id=1, source_target_pairs={{0,1},{1,0},{2,3},{3,2},{4,5},{5,4},{6,7},{7,6},{8,9},{9,8},{10,11... | collective-permute-start | bytes 1572872 | tf_op jit(solution)/shard_map/ppermute | solution.py:47
  71.2 14.2 %collective-permute-start.16 = (bf16[12,128,128]{2,1,0:T(8,128)(2,1)}, bf16[12,128,128]{2,1,0:T(8,128)(2,1)S(1)}, u32[]{:S(2)}, u32[]{:S(2)}) collective-permute-start(bf16[12,128,128]{2,1,0:T(8,128)(2,1)} %pad_maximum_fusion), channel_id=1, source_target_pairs={{0,2},{1,3},{2,0},{3,1},{4,6},{5,7},{6,4},{7,5},{8,10},{9,11},{10,... | collective-permute-start | bytes 1179656 | tf_op jit(solution)/shard_map/ppermute | solution.py:47
  74.4 11.9 %copy-start.19 = (f32[2,64]{1,0:T(2,128)S(1)}, f32[2,64]{1,0:T(2,128)}, u32[]{:S(2)}) copy-start(f32[2,64]{1,0:T(2,128)} %get-tuple-element.38) | copy-start | bytes 1540
  74.4 11.9 %copy-start.20 = (f32[2,64]{1,0:T(2,128)S(1)}, f32[2,64]{1,0:T(2,128)}, u32[]{:S(2)}) copy-start(f32[2,64]{1,0:T(2,128)} %get-tuple-element.39) | copy-start | bytes 1540
  74.4 11.9 %copy-start.21 = (f32[2,64]{1,0:T(2,128)S(1)}, f32[2,64]{1,0:T(2,128)}, u32[]{:S(2)}) copy-start(f32[2,64]{1,0:T(2,128)} %get-tuple-element.40) | copy-start | bytes 1540
  81.9 8.5 %collective-permute-start.12 = (bf16[128,512]{1,0:T(8,128)(2,1)}, bf16[128,512]{1,0:T(8,128)(2,1)S(1)}, u32[]{:S(2)}, u32[]{:S(2)}) collective-permute-start(bf16[128,512]{1,0:T(8,128)(2,1)} %get-tuple-element.19), channel_id=1, source_target_pairs={{0,18},{1,19},{2,16},{3,17},{4,22},{5,23},{6,20},{7,21},{8,26},{9,... | collective-permute-start | bytes 393224 | tf_op jit(solution)/shard_map/ppermute | solution.py:47
  83.4 7.9 %collective-permute-start.11 = (bf16[128,512]{1,0:T(8,128)(2,1)}, bf16[128,512]{1,0:T(8,128)(2,1)S(1)}, u32[]{:S(2)}, u32[]{:S(2)}) collective-permute-start(bf16[128,512]{1,0:T(8,128)(2,1)} %get-tuple-element.18), channel_id=1, source_target_pairs={{0,2},{1,3},{2,0},{3,1},{4,6},{5,7},{6,4},{7,5},{8,10},{9,11},{10,... | collective-permute-start | bytes 393224 | tf_op jit(solution)/shard_map/ppermute | solution.py:47
  84.1 7.3 %copy-start.10 = (f32[128,512]{1,0:T(8,128)S(1)}, f32[128,512]{1,0:T(8,128)}, u32[]{:S(2)}) copy-start(f32[128,512]{1,0:T(8,128)} %get-tuple-element.16) | copy-start | bytes 786436
  84.1 7.3 %copy-start.23 = (f32[128]{0:T(128)S(1)}, f32[128]{0:T(128)}, u32[]{:S(2)}) copy-start(f32[128]{0:T(128)} %add_rsqrt_fusion.1) | copy-start | bytes 1540
  84.1 7.3 %collective-permute-start.10 = (bf16[128,512]{1,0:T(8,128)(2,1)}, bf16[128,512]{1,0:T(8,128)(2,1)S(1)}, u32[]{:S(2)}, u32[]{:S(2)}) collective-permute-start(bf16[128,512]{1,0:T(8,128)(2,1)} %get-tuple-element.17), channel_id=1, source_target_pairs={{0,16},{1,17},{2,18},{3,19},{4,20},{5,21},{6,22},{7,23},{8,24},{9,... | collective-permute-start | bytes 393224 | tf_op jit(solution)/shard_map/ppermute | solution.py:47
  86.2 6.5 %collective-permute-start.17 = (bf16[24,128,128]{2,1,0:T(8,128)(2,1)}, bf16[24,128,128]{2,1,0:T(8,128)(2,1)S(1)}, u32[]{:S(2)}, u32[]{:S(2)}) collective-permute-start(bf16[24,128,128]{2,1,0:T(8,128)(2,1)} %constant_dynamic-update-slice_fusion), channel_id=1, source_target_pairs={{0,1},{1,0},{2,3},{3,2},{4,5},{5,4},{6,7},{7,6},{8,9},{9,8},{10,11... | collective-permute-start | bytes 2359304 | tf_op jit(solution)/shard_map/ppermute | solution.py:47
  89.2 2.6 %copy-start.12 = (f32[128,128]{1,0:T(8,128)S(1)}, f32[128,128]{1,0:T(8,128)}, u32[]{:S(2)}) copy-start(f32[128,128]{1,0:T(8,128)} %get-tuple-element.52) | copy-start | bytes 196612
  91.5 1.8 %copy-start.1 = (f32[128,512]{1,0:T(8,128)}, f32[128,512]{1,0:T(8,128)S(1)}, u32[]{:S(2)}) copy-start(f32[128,512]{1,0:T(8,128)S(1)} %add_multiply_fusion) | copy-start | bytes 786436
  91.6 1.7 %copy-start.9 = (bf16[3,16384]{1,0:T(4,128)(2,1)S(1)}, bf16[3,16384]{1,0:T(4,128)(2,1)}, u32[]{:S(2)}) copy-start(bf16[3,16384]{1,0:T(4,128)(2,1)} %fusion.5) | copy-start | bytes 294916
  106.6 8.8 %copy-start.15 = (s32[32]{0:T(128)S(1)}, s32[32]{0:T(128)}, u32[]{:S(2)}) copy-start(s32[32]{0:T(128)} %fusion.31) | copy-start | bytes 388
  106.6 9.4 %copy-start.13 = (f32[32,128]{1,0:T(8,128)S(1)}, f32[32,128]{1,0:T(8,128)}, u32[]{:S(2)}) copy-start(f32[32,128]{1,0:T(8,128)} %get-tuple-element.54) | copy-start | bytes 49156
  115.4 15.5 %copy-start.11 = (f32[128,128]{1,0:T(8,128)S(1)}, f32[128,128]{1,0:T(8,128)}, u32[]{:S(2)}) copy-start(f32[128,128]{1,0:T(8,128)} %get-tuple-element.51) | copy-start | bytes 196612
  115.4 15.5 %copy-start.2 = (f32[128,512]{1,0:T(8,128)S(1)}, f32[128,512]{1,0:T(8,128)}, u32[]{:S(2)}) copy-start(f32[128,512]{1,0:T(8,128)} %copy-done.1) | copy-start | bytes 786436
  115.4 15.5 %copy-start.5 = (f32[128,4,128]{2,1,0:T(4,128)S(1)}, f32[128,4,128]{2,1,0:T(4,128)}, u32[]{:S(2)}) copy-start(f32[128,4,128]{2,1,0:T(4,128)} %maximum_multiply_fusion) | copy-start | bytes 786436
  115.7 22.8 %copy-start.17 = (f32[2,128]{1,0:T(2,128)S(1)}, f32[2,128]{1,0:T(2,128)}, u32[]{:S(2)}) copy-start(f32[2,128]{1,0:T(2,128)} %get-tuple-element.55) | copy-start | bytes 3076
  115.7 22.8 %copy-start.18 = (f32[2,128]{1,0:T(2,128)S(1)}, f32[2,128]{1,0:T(2,128)}, u32[]{:S(2)}) copy-start(f32[2,128]{1,0:T(2,128)} %get-tuple-element.56) | copy-start | bytes 3076
  115.8 22.9 %copy-start.8 = (bf16[2,4,256,128]{3,2,1,0:T(8,128)(2,1)S(1)}, bf16[2,4,256,128]{3,2,1,0:T(8,128)(2,1)}, u32[]{:S(2)}) copy-start(bf16[2,4,256,128]{3,2,1,0:T(8,128)(2,1)} %param.17) | copy-start | bytes 1572868
  115.8 22.9 %copy-start.22 = (pred[2,256]{1,0:T(4,128)(4,1)S(1)}, pred[2,256]{1,0:T(4,128)(4,1)}, u32[]{:S(2)}) copy-start(pred[2,256]{1,0:T(4,128)(4,1)} %iota_compare_fusion.4) | copy-start | bytes 1540
  116.2 22.9 %copy-start.25 = (bf16[2,4,256,128]{3,2,1,0:T(8,128)(2,1)S(1)}, bf16[2,4,256,128]{3,2,1,0:T(8,128)(2,1)}, u32[]{:S(2)}) copy-start(bf16[2,4,256,128]{3,2,1,0:T(8,128)(2,1)} %param.18) | copy-start | bytes 1572868
  116.9 21.3 %all-to-all-start = ((bf16[16,2,1536]{2,1,0:T(2,128)(2,1)}), bf16[16,2,1536]{2,1,0:T(2,128)(2,1)S(1)}, u32[]{:S(2)}, u32[]{:S(2)}) async-start(bf16[16,2,1536]{2,1,0:T(2,128)(2,1)} %reshape.225), calls=%async_computation | async-start | bytes 196608 | tf_op jit(solution)/shard_map/all_to_all | solution.py:287
